TPU v7x, 32 devices: a whole 2x2x4 slice. The times are simulated.
32 devices in a mesh: slab: 32 (over z, y, x, core).
Axes of the slice: x: 2, y: 2, z: 4, core: 2. Of those that a mesh axis runs over, the one named last changes fastest.
Arguments:
- series: float32 [80, 1048576], P(None, 'slab'), as said below
- noise_mask: int32 [1048576], P('slab'), may hold values 0 or 1
- probes: float32 [80, 5], replicated, may hold values from -6 to 6
- sample_weights: bfloat16 [1536, 256, 128], P('slab'), may hold values from -0.375 to 0.375
- block_ids: int32 [1536], P('slab'), may hold values from 0 to 127
- tile_ids: int32 [1536], P('slab'), may hold values from -1 to 127, as said below
- tile_owner: int32 [128], replicated, may hold values from 0 to 31, as said below
Outputs:
- vertex_series: float32 [128, 80, 128], P('slab')
Inputs may be any that keep to these rules, and one draw needn't show every extreme that they name: `tile_ids`: on each device the used entries come first and are at least half of its 48 entries; some device uses all. Used entry k of the device with index d names vertex tile (d * 4 + o_d + k) mod 128, with o_d in [0, 4) fixed per device; unused entries hold -1. tile_owner[j] = p[j mod the number of devices] for a permutation p of the devices, so every device owns 4 tiles. `series`: values of order one to some tens; each voxel carries its own baseline.
All inputs are finite; a program needn't handle non-finite values. No bound on the sum of `noise_mask` on one device may be relied on, other than what follows from the above.
Results may differ from a plain program's by a relative error of at most 0.005.
Values may be sent and summed in bfloat16 or wider, within the bound.
No kernel may reach another device: no remote copies, remote signals or barrier semaphores. Data moves between devices by JAX's collectives and lax.ppermute only.
A program may use at most 128 MiB of HBM per device.

v0:
```python
import jax
import jax.numpy as jnp
from jax import lax
from jax.sharding import PartitionSpec as P

HIGHEST = lax.Precision.HIGHEST


def make_projector(components):
    inner = jnp.dot(components.T, components, precision=HIGHEST)
    factor = jnp.linalg.cholesky(inner)
    solved = jax.scipy.linalg.cho_solve((factor, True), components.T)
    return jnp.dot(components, solved, precision=HIGHEST)


def body(series, noise_mask, probes, sample_weights, block_ids, tile_ids, tile_owner):
    frames, voxels = series.shape
    devices = lax.axis_size("slab")
    tile_width = sample_weights.shape[2]
    block_width = sample_weights.shape[1]
    owned = tile_owner.shape[0] // devices
    demeaned = series - jnp.mean(series, axis=0, keepdims=True)
    weighted = demeaned * noise_mask.astype(jnp.float32)[None, :]
    local_gram = lax.dot_general(weighted, demeaned, (((1,), (1,)), ((), ())), precision=HIGHEST)
    noise_gram = lax.psum(local_gram, "slab")
    components = jnp.dot(noise_gram, probes, precision=HIGHEST)
    projector = make_projector(components)
    cleaned = (demeaned - jnp.dot(projector, demeaned, precision=HIGHEST)).astype(jnp.bfloat16)
    blocks = cleaned.reshape(frames, voxels // block_width, block_width)
    picked = jnp.take(blocks, block_ids, axis=1)
    partial_value = jnp.einsum(
        "fkv,kvt->kft", picked, sample_weights, preferred_element_type=jnp.float32
    ).astype(jnp.bfloat16)
    used = tile_ids >= 0
    matches = tile_ids[:, None] == jnp.arange(tile_owner.shape[0], dtype=jnp.int32)[None, :]
    owners = jnp.sum(jnp.where(matches, tile_owner[None, :], 0), axis=1)
    local_slot = jnp.where(used, tile_ids // devices, -1)
    total_rows = owned * devices
    rows = jnp.where(used, owners * owned + local_slot, total_rows)
    widened = partial_value.astype(jnp.float32)
    inside = (rows >= 0) & (rows < owned * lax.axis_size("slab"))
    target = jnp.where(inside, rows, owned * lax.axis_size("slab"))
    empty = jnp.zeros((owned * lax.axis_size("slab"), frames, tile_width), jnp.float32)
    return lax.psum_scatter(
        empty.at[target].add(widened, mode="drop"), "slab", scatter_dimension=0, tiled=True
    )


def solution(mesh):
    return jax.shard_map(
        body,
        mesh=mesh,
        in_specs=(
            P(None, "slab"),
            P("slab"),
            P(),
            P("slab", None, None),
            P("slab"),
            P("slab"),
            P(),
        ),
        out_specs=P("slab", None, None),
        check_vma=False,
    )
```

profile of v0, /device:TPU:0, one launch (start us, length us, event | category | flops | bytes accessed | tf_op | source)
XLA Modules:
  0.0 259.4 jit_solution(14531749879565290467)
XLA Ops:
  6.5 0.0 copy-start
  6.5 0.0 reduce-scatter.2.cloned.1.call-start
  6.5 0.8 compare_and_fusion
  7.4 0.8 compare_select_fusion
  8.2 0.8 select_reduce_fusion
  9.0 0.7 compare_select_fusion.1
  9.7 0.9 convert_element_type.12
  10.6 4.7 %reduce_sum.19 = f32[32768]{0:T(1024)S(1)} reduce(f32[80,32768]{1,0:T(8,128)} %param.7, f32[]{:T(128)} %constant.78.clone.1), dimensions={0}, to_apply=%region_1.0 | reduce | flops 2588672 | bytes 10616836 | tf_op jit(solution)/shard_map/reduce_sum | solution.py:22
  15.3 0.0 copy-start.1
  15.3 13.9 %fusion.1 = f32[80,80]{1,0:T(8,128)S(1)} fusion(f32[80,32768]{1,0:T(8,128)} %param.7, f32[32768]{0:T(1024)S(1)} %convert_element_type.12, f32[32768]{0:T(1024)S(1)} %broadcast_multiply_fusion), kind=kOutput, calls=%fused_computation.4 | convolution fusion | flops 2524446720 | bytes 10773504 | tf_op jit(solution)/shard_map/dot_general | solution.py:24
  29.2 42.6 %psum.7 = f32[80,80]{1,0:T(8,128)S(1)} all-reduce(f32[80,80]{1,0:T(8,128)S(1)} %fusion.1), channel_id=1, replica_groups=mesh['slab'=32] {'slab'}, use_global_device_ids=true, to_apply=%region_2.3 | all-reduce | flops 6400 | bytes 51200 | tf_op jit(solution)/shard_map/psum | solution.py:25
  71.8 0.0 copy-done.1
  71.8 0.2 fusion.27
  71.9 0.2 fusion.28
  72.1 0.1 copy.13
  72.2 0.4 cholesky.16
  72.6 0.1 select_reduce_fusion.1
  72.7 0.6 compare_reduce_fusion
  73.3 0.6 fusion.19
  74.0 0.4 custom-call.10
  74.4 0.2 fusion.20
  74.6 0.1 fusion.22
  74.7 0.3 fusion.29
  75.0 12.9 %fusion = bf16[80,32768]{1,0:T(8,128)(2,1)S(1)} fusion(f32[80,80]{1,0:T(8,128)S(1)} %fusion.29, f32[80,32768]{1,0:T(8,128)} %param.7, f32[32768]{0:T(1024)S(1)} %broadcast_multiply_fusion), kind=kOutput, calls=%fused_computation.3 | convolution fusion | flops 2524446720 | bytes 15885312 | tf_op jit(solution)/shard_map/dot_general | solution.py:28
  87.9 2.8 %copy.18 = bf16[10,128,8,256]{3,2,0,1:T(8,128)(2,1)} copy(bf16[10,128,8,256]{3,2,1,0:T(8,128)(2,1)S(1)} %bitcast.34) | data formatting | bytes 10485760 | tf_op jit(solution)/shard_map/reshape | solution.py:29
  90.7 4.5 %gather_fusion = bf16[48,80,256]{2,1,0:T(8,128)(2,1)} fusion(bf16[80,128,256]{2,0,1:T(8,128)(2,1)} %bitcast.35, s32[1024]{0:T(1024)S(1)} %pad_clamp_fusion), kind=kCustom, calls=%fused_computation | custom fusion | bytes 3932352 | tf_op jit(solution)/shard_map/jit(_take)/gather | solution.py:30
  95.2 0.0 copy-done
  95.2 3.7 %fusion.15 = f32[48,80,128]{2,1,0:T(8,128)} fusion(bf16[48,256,128]{2,1,0:T(8,128)(2,1)S(1)} %copy-done, bf16[48,80,256]{2,1,0:T(8,128)(2,1)} %gather_fusion, pred[48]{0:T(512)(128)(4,1)S(1)} %compare_and_fusion), kind=kOutput, calls=%fused_computation.17 | convolution fusion | flops 253624320 | bytes 7077936 | tf_op jit(solution)/shard_map/fkv,kvt->kft/dot_general | solution.py:31
  98.9 2.7 %broadcast_in_dim.41 = f32[128,80,128]{2,1,0:T(8,128)} broadcast(f32[]{:T(128)} %constant.78.clone.1), dimensions={} | broadcast | bytes 5242884 | tf_op jit(solution)/shard_map/broadcast_in_dim | solution.py:43
  101.5 8.2 %scatter_fusion = f32[128,80,128]{2,1,0:T(8,128)} fusion(f32[128,80,128]{2,1,0:T(8,128)} %broadcast_in_dim.41, s32[48]{0:T(128)S(1)} %compare_select_fusion.1, f32[48,80,128]{2,1,0:T(8,128)} %fusion.15), kind=kCustom, calls=%fused_computation.1 | custom fusion | flops 491520 | bytes 5898432 | tf_op jit(solution)/shard_map/scatter-add | solution.py:45
  109.8 0.0 reduce-scatter.2.cloned.1.call-update
  109.8 142.7 %reduce-scatter.2.cloned.1.call-done = f32[4,80,128]{2,1,0:T(8,128)} async-done(((f32[128,80,128]{2,1,0:T(8,128)}), f32[4,80,128]{2,1,0:T(8,128)}) %reduce-scatter.2.cloned.1.call-update) | async-done | bytes 163856 | tf_op jit(solution)/shard_map/reduce_scatter | solution.py:44
  (3 shorter events, 0.0 us)
Async XLA Ops:
  6.5 88.7 %copy-start = (bf16[48,256,128]{2,1,0:T(8,128)(2,1)S(1)}, bf16[48,256,128]{2,1,0:T(8,128)(2,1)}, u32[]{:S(2)}) copy-start(bf16[48,256,128]{2,1,0:T(8,128)(2,1)} %param.10) | copy-start | bytes 9437188
  6.5 246.0 %reduce-scatter.2.cloned.1.call-start = ((), (), s32[]{:S(2)}) async-start(), calls=%async_computation.1 | async-start | bytes 5406720 | tf_op jit(solution)/shard_map/reduce_scatter | solution.py:44
  15.3 56.5 %copy-start.1 = (f32[80,5]{0,1:T(8,128)S(1)}, f32[80,5]{0,1:T(8,128)}, u32[]{:S(2)}) copy-start(f32[80,5]{0,1:T(8,128)} %param.9) | copy-start | bytes 4804
Sparse Core Ops, SparseCore 0:
  109.9 142.5 reduce-scatter.1
where the time goes:
time: 260 us; the launch traced here: 259 us
  waiting for transfers between devices  143 us (55%)
  blocking collectives  42.6 us (16%)
  matrix products  31.4 us (12%)
  other arithmetic  19.2 us (7%)
  between operations  13.5 us (5%)
  local copies, waits for them, and re-layouts  10 us (4%)
    reduce_scatter x1, waiting for transfers between devices, body(): lax.psum_scatter(empty.at[target].add(widened, mode='drop'), 'slab', scat...  143 us
    psum x1, blocking collectives, body(): noise_gram = lax.psum(local_gram, 'slab')  42.6 us
    dot_general x1, matrix products, body(): lax.dot_general(weighted, demeaned, (((1,), (1,)), ((), ())), precision=H...  13.9 us
    dot_general x1, matrix products, body(): jnp.dot(projector, demeaned, precision=HIGHEST)  12.9 us
    scatter-add x1, other arithmetic, body(): empty.at[target].add(widened, mode='drop')  8.25 us
  transfers between devices with their start and end apart: 1, of which 1 were waited for; matrix products, arithmetic and copies ran while one was open for 0% of the time, Pallas kernels for 0%

commit v1 on v0

--- a/solution.py
+++ b/solution.py
@@ -22,7 +22,11 @@
     demeaned = series - jnp.mean(series, axis=0, keepdims=True)
     weighted = demeaned * noise_mask.astype(jnp.float32)[None, :]
     local_gram = lax.dot_general(weighted, demeaned, (((1,), (1,)), ((), ())), precision=HIGHEST)
-    noise_gram = lax.psum(local_gram, "slab")
+    noise_gram = local_gram
+    for hop in (1, 2, 4, 8, 16):
+        noise_gram = noise_gram + lax.ppermute(
+            noise_gram, "slab", [(dev, dev ^ hop) for dev in range(32)]
+        )
     components = jnp.dot(noise_gram, probes, precision=HIGHEST)
     projector = make_projector(components)
     cleaned = (demeaned - jnp.dot(projector, demeaned, precision=HIGHEST)).astype(jnp.bfloat16)

time: 260 us -> 236 us (0.908)
  blocking collectives: 42.6 us -> 0 us
  waiting for transfers between devices: 143 us -> 154 us
  starting transfers between devices: 0.01 us -> 10.6 us
  other arithmetic: 19.2 us -> 16.4 us
    psum x1 -> x0, blocking collectives: 42.6 us -> none  [body(): noise_gram = lax.psum(local_gram, 'slab')]
    ppermute x0 -> x5, starting transfers between devices: none -> 10.6 us  [body(): lax.ppermute(noise_gram, 'slab', [(dev, dev ^ hop) for dev in range(32)])]
    ppermute x0 -> x5, waiting for transfers between devices: none -> 8.57 us  [body(): lax.ppermute(noise_gram, 'slab', [(dev, dev ^ hop) for dev in range(32)])]
  transfers between devices with their start and end apart: 1 -> 6, of which waited for: 1 -> 6; matrix products, arithmetic and copies ran while one was open for 0% -> 0% of each run, Pallas kernels for 0% -> 0%
where the time goes in v1:
time: 236 us
  waiting for transfers between devices  154 us (65%)
  matrix products  31.6 us (13%)
  other arithmetic  16.4 us (7%)
  between operations  13.5 us (6%)
  starting transfers between devices  10.6 us (4%)
  local copies, waits for them, and re-layouts  10.1 us (4%)
    reduce_scatter x1, waiting for transfers between devices, body(): lax.psum_scatter(empty.at[target].add(widened, mode='drop'), 'slab', scat...  145 us
    dot_general x1, matrix products, body(): lax.dot_general(weighted, demeaned, (((1,), (1,)), ((), ())), precision=H...  13.9 us
    dot_general x1, matrix products, body(): jnp.dot(projector, demeaned, precision=HIGHEST)  13.1 us
    ppermute x5, starting transfers between devices, body(): lax.ppermute(noise_gram, 'slab', [(dev, dev ^ hop) for dev in range(32)])  10.6 us
    ppermute x5, waiting for transfers between devices, body(): lax.ppermute(noise_gram, 'slab', [(dev, dev ^ hop) for dev in range(32)])  8.57 us
    scatter-add x1, other arithmetic, body(): empty.at[target].add(widened, mode='drop')  8.25 us
  transfers between devices with their start and end apart: 6, of which 6 were waited for; matrix products, arithmetic and copies ran while one was open for 0% of the time, Pallas kernels for 0%

profile of v1, /device:TPU:0, one launch (start us, length us, event | category | flops | bytes accessed | tf_op | source)
XLA Modules:
  0.0 236.0 jit_solution(5771365312990590895)
XLA Ops:
  6.5 0.0 copy-start
  6.5 0.0 reduce-scatter.2.cloned.1.call-start
  6.5 1.1 convert_element_type.12
  7.6 4.7 %reduce_sum.19 = f32[32768]{0:T(1024)S(1)} reduce(f32[80,32768]{1,0:T(8,128)} %param.7, f32[]{:T(128)} %constant.78.clone.1), dimensions={0}, to_apply=%region_1.2 | reduce | flops 2588672 | bytes 10616836 | tf_op jit(solution)/shard_map/reduce_sum | solution.py:22
  12.3 0.0 copy-start.2
  12.3 0.0 copy-start.3
  12.3 0.0 copy-start.4
  12.3 0.0 copy-start.1
  12.3 13.9 %fusion.1 = f32[80,80]{1,0:T(8,128)S(1)} fusion(f32[80,32768]{1,0:T(8,128)} %param.7, f32[32768]{0:T(1024)S(1)} %convert_element_type.12, f32[32768]{0:T(1024)S(1)} %broadcast_multiply_fusion), kind=kOutput, calls=%fused_computation.4 | convolution fusion | flops 2524446720 | bytes 10773504 | tf_op jit(solution)/shard_map/dot_general | solution.py:24
  26.2 0.5 collective-permute-start
  26.8 0.0 copy-done.2
  26.8 0.0 copy-done.3
  26.8 0.2 select_reduce_fusion
  26.9 0.7 collective-permute-done
  27.6 2.8 %collective-permute-start.1 = (f32[80,80]{1,0:T(8,128)S(1)}, f32[80,80]{1,0:T(8,128)S(1)}, u32[]{:S(2)}, u32[]{:S(2)}) collective-permute-start(f32[80,80]{1,0:T(8,128)S(1)} %add.50), channel_id=1, source_target_pairs={{0,2},{1,3},{2,0},{3,1},{4,6},{5,7},{6,4},{7,5},{8,10},{9,11},{10,... | collective-permute-start | bytes 76808 | tf_op jit(solution)/shard_map/ppermute | solution.py:27
  30.5 2.0 collective-permute-done.1
  32.5 2.1 collective-permute-start.2
  34.5 0.0 copy-done.4
  34.5 2.0 collective-permute-done.2
  36.5 2.1 collective-permute-start.3
  38.6 2.0 collective-permute-done.3
  40.6 3.1 %collective-permute-start.4 = (f32[80,80]{1,0:T(8,128)S(1)}, f32[80,80]{1,0:T(8,128)S(1)}, u32[]{:S(2)}, u32[]{:S(2)}) collective-permute-start(f32[80,80]{1,0:T(8,128)S(1)} %add.53), channel_id=1, source_target_pairs={{0,16},{1,17},{2,18},{3,19},{4,20},{5,21},{6,22},{7,23},{8,24},{9,... | collective-permute-start | bytes 76808 | tf_op jit(solution)/shard_map/ppermute | solution.py:27
  43.7 2.0 collective-permute-done.4
  45.6 0.0 copy-done.1
  45.7 0.2 fusion.19
  45.8 0.2 fusion.29
  46.0 0.1 copy.13
  46.1 0.4 cholesky.16
  46.5 0.1 select_reduce_fusion.1
  46.6 0.6 compare_reduce_fusion
  47.2 0.6 fusion.21
  47.9 0.4 custom-call.10
  48.3 0.2 fusion.22
  48.4 0.1 fusion.24
  48.6 0.3 fusion.30
  48.9 13.1 %fusion = bf16[80,32768]{1,0:T(8,128)(2,1)S(1)} fusion(f32[80,80]{1,0:T(8,128)S(1)} %fusion.30, f32[80,32768]{1,0:T(8,128)} %param.7, f32[32768]{0:T(1024)S(1)} %broadcast_multiply_fusion), kind=kOutput, calls=%fused_computation.3 | convolution fusion | flops 2524446720 | bytes 15885312 | tf_op jit(solution)/shard_map/dot_general | solution.py:32
  62.0 2.8 %copy.18 = bf16[10,128,8,256]{3,2,0,1:T(8,128)(2,1)} copy(bf16[10,128,8,256]{3,2,1,0:T(8,128)(2,1)S(1)} %bitcast.33) | data formatting | bytes 10485760 | tf_op jit(solution)/shard_map/reshape | solution.py:33
  64.7 4.5 %gather_fusion = bf16[48,80,256]{2,1,0:T(8,128)(2,1)} fusion(bf16[80,128,256]{2,0,1:T(8,128)(2,1)} %bitcast.34, s32[1024]{0:T(1024)S(1)} %pad_clamp_fusion), kind=kCustom, calls=%fused_computation | custom fusion | bytes 3932352 | tf_op jit(solution)/shard_map/jit(_take)/gather | solution.py:34
  69.3 0.0 copy-done
  69.3 3.7 %fusion.15 = f32[48,80,128]{2,1,0:T(8,128)} fusion(bf16[48,256,128]{2,1,0:T(8,128)(2,1)S(1)} %copy-done, bf16[48,80,256]{2,1,0:T(8,128)(2,1)} %gather_fusion, pred[48]{0:T(512)(128)(4,1)S(1)} %compare_and_fusion), kind=kOutput, calls=%fused_computation.17 | convolution fusion | flops 253624320 | bytes 7077936 | tf_op jit(solution)/shard_map/fkv,kvt->kft/dot_general | solution.py:35
  72.9 2.7 %broadcast_in_dim.41 = f32[128,80,128]{2,1,0:T(8,128)} broadcast(f32[]{:T(128)} %constant.78.clone.1), dimensions={} | broadcast | bytes 5242884 | tf_op jit(solution)/shard_map/broadcast_in_dim | solution.py:47
  75.6 8.2 %scatter_fusion = f32[128,80,128]{2,1,0:T(8,128)} fusion(f32[128,80,128]{2,1,0:T(8,128)} %broadcast_in_dim.41, s32[48]{0:T(128)S(1)} %compare_select_fusion.1, f32[48,80,128]{2,1,0:T(8,128)} %fusion.15), kind=kCustom, calls=%fused_computation.1 | custom fusion | flops 491520 | bytes 5898432 | tf_op jit(solution)/shard_map/scatter-add | solution.py:49
  83.9 0.0 reduce-scatter.2.cloned.1.call-update
  83.9 145.3 %reduce-scatter.2.cloned.1.call-done = f32[4,80,128]{2,1,0:T(8,128)} async-done(((f32[128,80,128]{2,1,0:T(8,128)}), f32[4,80,128]{2,1,0:T(8,128)}) %reduce-scatter.2.cloned.1.call-update) | async-done | bytes 163856 | tf_op jit(solution)/shard_map/reduce_scatter | solution.py:48
  (10 shorter events, 0.1 us)
Async XLA Ops:
  6.5 62.7 %copy-start = (bf16[48,256,128]{2,1,0:T(8,128)(2,1)S(1)}, bf16[48,256,128]{2,1,0:T(8,128)(2,1)}, u32[]{:S(2)}) copy-start(bf16[48,256,128]{2,1,0:T(8,128)(2,1)} %param.10) | copy-start | bytes 9437188
  6.5 222.6 %reduce-scatter.2.cloned.1.call-start = ((), (), s32[]{:S(2)}) async-start(), calls=%async_computation.1 | async-start | bytes 5406720 | tf_op jit(solution)/shard_map/reduce_scatter | solution.py:48
  12.3 14.5 %copy-start.2 = (s32[128]{0:T(128)S(1)}, s32[128]{0:T(128)}, u32[]{:S(2)}) copy-start(s32[128]{0:T(128)} %param.13) | copy-start | bytes 1540
  12.3 14.4 %copy-start.3 = (s32[48]{0:T(128)S(1)}, s32[48]{0:T(128)}, u32[]{:S(2)}) copy-start(s32[48]{0:T(128)} %param.12) | copy-start | bytes 580
  12.3 22.2 %copy-start.4 = (s32[48]{0:T(128)S(1)}, s32[48]{0:T(128)}, u32[]{:S(2)}) copy-start(s32[48]{0:T(128)} %param.11) | copy-start | bytes 580
  12.3 33.3 %copy-start.1 = (f32[80,5]{0,1:T(8,128)S(1)}, f32[80,5]{0,1:T(8,128)}, u32[]{:S(2)}) copy-start(f32[80,5]{0,1:T(8,128)} %param.9) | copy-start | bytes 4804
  26.2 1.4 collective-permute-start
  27.6 4.8 %collective-permute-start.1 = (f32[80,80]{1,0:T(8,128)S(1)}, f32[80,80]{1,0:T(8,128)S(1)}, u32[]{:S(2)}, u32[]{:S(2)}) collective-permute-start(f32[80,80]{1,0:T(8,128)S(1)} %add.50), channel_id=1, source_target_pairs={{0,2},{1,3},{2,0},{3,1},{4,6},{5,7},{6,4},{7,5},{8,10},{9,11},{10,... | collective-permute-start | bytes 76808 | tf_op jit(solution)/shard_map/ppermute | solution.py:27
  32.5 4.0 %collective-permute-start.2 = (f32[80,80]{1,0:T(8,128)S(1)}, f32[80,80]{1,0:T(8,128)S(1)}, u32[]{:S(2)}, u32[]{:S(2)}) collective-permute-start(f32[80,80]{1,0:T(8,128)S(1)} %add.51), channel_id=1, source_target_pairs={{0,4},{1,5},{2,6},{3,7},{4,0},{5,1},{6,2},{7,3},{8,12},{9,13},{10,... | collective-permute-start | bytes 76808 | tf_op jit(solution)/shard_map/ppermute | solution.py:27
  36.5 4.1 %collective-permute-start.3 = (f32[80,80]{1,0:T(8,128)S(1)}, f32[80,80]{1,0:T(8,128)S(1)}, u32[]{:S(2)}, u32[]{:S(2)}) collective-permute-start(f32[80,80]{1,0:T(8,128)S(1)} %add.52), channel_id=1, source_target_pairs={{0,8},{1,9},{2,10},{3,11},{4,12},{5,13},{6,14},{7,15},{8,0},{9,1},... | collective-permute-start | bytes 76808 | tf_op jit(solution)/shard_map/ppermute | solution.py:27
  40.6 5.1 %collective-permute-start.4 = (f32[80,80]{1,0:T(8,128)S(1)}, f32[80,80]{1,0:T(8,128)S(1)}, u32[]{:S(2)}, u32[]{:S(2)}) collective-permute-start(f32[80,80]{1,0:T(8,128)S(1)} %add.53), channel_id=1, source_target_pairs={{0,16},{1,17},{2,18},{3,19},{4,20},{5,21},{6,22},{7,23},{8,24},{9,... | collective-permute-start | bytes 76808 | tf_op jit(solution)/shard_map/ppermute | solution.py:27
Sparse Core Ops, SparseCore 0:
  84.0 145.1 reduce-scatter.1
